TPU v7x, 128 devices: a whole 4x4x4 slice. The times are simulated.
128 devices in a mesh: ctx: 32 (over z, y, core), head: 4 (over x).
Axes of the slice: x: 4, y: 4, z: 4, core: 2. Of those that a mesh axis runs over, the one named last changes fastest.
Arguments:
- inputs: bfloat16 [32768, 8192], P(('ctx', 'head')), may hold values from -6 to 6
- out_grad: bfloat16 [32768, 8192], P(('ctx', 'head')), may hold values from -0.59765625 to 0.59765625
- input_map: bfloat16 [32768, 1024], P(('ctx', 'head')), may hold values from -0.52734375 to 0.52734375
- output_map: bfloat16 [32768, 1024], P(('ctx', 'head')), may hold values from -0.52734375 to 0.52734375
- log_decay: float32 [32768, 128], P(('ctx', 'head')), may hold values from -1 to 0, as said below
- block_mask: int32 [256, 256], replicated, may hold values from 0 to 1, as said below
Outputs:
- grad_inputs: bfloat16 [32768, 8192], P(('ctx', 'head'))
- grad_input_map: bfloat16 [32768, 1024], P(('ctx', 'head'))
- grad_output_map: bfloat16 [32768, 1024], P(('ctx', 'head'))
- grad_log_decay: float32 [32768, 128], P(('ctx', 'head'))
Inputs may be any that keep to these rules, and one draw needn't show every extreme that they name: `log_decay`: every entry is negative. `block_mask`: inside each of the 16 diagonal tiles of 16 rows the mask is 1 on and below the diagonal and 0 above it; every tile below the diagonal tiles is all ones or all zeros; tiles above them are zeros.
All inputs are finite; a program needn't handle non-finite values.
Results may differ from a plain program's by a relative error of at most 0.004.
Values may be sent and summed in bfloat16 or wider, within the bound.
A program may use at most 256 MiB of HBM per device.

v0:
```python
from functools import partial

import jax
import jax.numpy as jnp
from jax import lax
from jax.sharding import PartitionSpec as P

HEAD_COUNT = 128
HEAD_DIM = 64
STATE = 128
GROUPS = 8
BLOCK = 256


HIGHEST_PRECISION = lax.Precision.HIGHEST


def entering_2(part, axis, combine, identity, reverse):
    count = lax.axis_size(axis)
    place = lax.axis_index(axis)
    ahead = count - 1 - place if reverse else place
    gathered = jax.tree.map(lambda a: lax.all_gather(a, axis), part)
    state = jax.tree.map(lambda a, e: jnp.zeros_like(a) + jnp.asarray(e, a.dtype), part, identity)

    def one(lap, state):
        source = count - 1 - lap if reverse else lap
        return combine(
            state, jax.tree.map(lambda a: lax.dynamic_index_in_dim(a, source, 0, False), gathered)
        )

    return lax.fori_loop(0, ahead, one, state)


def product_two(form, first, second):
    return jnp.einsum(
        form, first, second, precision=HIGHEST_PRECISION, preferred_element_type=jnp.float32
    )


def product_three(form, first, second, third):
    return jnp.einsum(
        form, first, second, third, precision=HIGHEST_PRECISION, preferred_element_type=jnp.float32
    )


def narrow_two(form, first, second):
    return jnp.einsum(form, first, second, preferred_element_type=jnp.float32)


def group_slices(inputs, out_grad, keys, queries, levels, cluster):
    per_group = HEAD_COUNT // GROUPS
    feature_span = per_group * HEAD_DIM
    token_count = inputs.shape[0]
    group_inputs = inputs[:, cluster * feature_span : (cluster + 1) * feature_span].reshape(
        token_count, per_group, HEAD_DIM
    )
    group_grads = out_grad[:, cluster * feature_span : (cluster + 1) * feature_span].reshape(
        token_count, per_group, HEAD_DIM
    )
    group_keys = keys[:, cluster * STATE : (cluster + 1) * STATE]
    group_query = queries[:, cluster * STATE : (cluster + 1) * STATE]
    group_level = levels[:, cluster * per_group : (cluster + 1) * per_group]
    return (group_inputs, group_grads, group_keys, group_query, group_level)


def block_summary(pieces):
    inputs, out_grad, keys, queries, levels = pieces
    clusters = keys.shape[1] // STATE
    written_parts = []
    read_parts = []
    for cluster in range(clusters):
        group_inputs, group_grads, group_keys, group_query, group_level = group_slices(
            inputs, out_grad, keys, queries, levels, cluster
        )
        closing = jnp.exp(group_level[-1:] - group_level)
        opening = jnp.exp(group_level)
        written_parts.append(
            product_three(
                "sn,sr,srp->rnp",
                group_keys.astype(jnp.float32),
                closing,
                group_inputs.astype(jnp.float32),
            )
        )
        read_parts.append(
            product_three(
                "tn,tr,trp->rnp",
                group_query.astype(jnp.float32),
                opening,
                group_grads.astype(jnp.float32),
            )
        )
    return (
        jnp.concatenate(written_parts, axis=0),
        jnp.concatenate(read_parts, axis=0),
        jnp.exp(levels[-1]),
    )


def block_grads(pieces, mask_values):
    inputs, out_grad, keys, queries, levels, state_in, grad_leave = pieces
    per_group = HEAD_COUNT // GROUPS
    clusters = keys.shape[1] // STATE
    token_count = inputs.shape[0]
    input_parts = []
    key_parts = []
    query_parts = []
    decay_parts = []
    for cluster in range(clusters):
        group_inputs, group_grads, group_keys, group_query, group_level = group_slices(
            inputs, out_grad, keys, queries, levels, cluster
        )
        inputs_wide = group_inputs.astype(jnp.float32)
        grads_wide = group_grads.astype(jnp.float32)
        keys_wide = group_keys.astype(jnp.float32)
        query_wide = group_query.astype(jnp.float32)
        group_state = state_in[cluster * per_group : (cluster + 1) * per_group]
        group_leave = grad_leave[cluster * per_group : (cluster + 1) * per_group]
        transposed = group_level.T
        weight = mask_values[None] * jnp.exp(
            jnp.minimum(transposed[:, :, None] - transposed[:, None, :], 0.0)
        )
        scores = narrow_two("tn,sn->ts", group_query, group_keys)
        pairing = narrow_two("trp,srp->rts", group_grads, group_inputs)
        weighted = weight * scores[None]
        grad_in = product_two("rts,trp->srp", weighted, grads_wide)
        masked = weight * pairing
        combined = jnp.sum(masked, axis=0)
        grad_query = product_two("ts,sn->tn", combined, keys_wide)
        grad_keys = product_two("ts,tn->sn", combined, query_wide)
        paired = masked * scores[None]
        grad_level = (jnp.sum(paired, axis=2) - jnp.sum(paired, axis=1)).T
        opening = jnp.exp(group_level)
        carried = product_two("tn,rnp->trp", query_wide, group_state)
        grad_level = grad_level + opening * jnp.sum(carried * grads_wide, axis=2)
        grad_query = grad_query + product_three("tr,trp,rnp->tn", opening, grads_wide, group_state)
        closing = jnp.exp(group_level[-1:] - group_level)
        inward = product_two("srp,rnp->srn", inputs_wide, group_leave)
        grad_keys = grad_keys + product_two("sr,srn->sn", closing, inward)
        touched = closing * product_two("sn,srn->sr", keys_wide, inward)
        grad_level = grad_level - touched
        ending = jnp.sum(touched, axis=0) + jnp.exp(group_level[-1]) * jnp.sum(
            group_state * group_leave, axis=(1, 2)
        )
        grad_level = grad_level.at[-1].add(ending)
        grad_decay = jnp.flip(jnp.cumsum(jnp.flip(grad_level, 0), axis=0), 0)
        grad_in = grad_in + closing[:, :, None] * product_two("sn,rnp->srp", keys_wide, group_leave)
        input_parts.append(grad_in.reshape(token_count, per_group * HEAD_DIM))
        key_parts.append(grad_keys)
        query_parts.append(grad_query)
        decay_parts.append(grad_decay)
    return (
        jnp.concatenate(input_parts, axis=1),
        jnp.concatenate(key_parts, axis=1),
        jnp.concatenate(query_parts, axis=1),
        jnp.concatenate(decay_parts, axis=1),
    )


def combine(earlier, latter):
    return (earlier[0] * latter[0], latter[1] + latter[0][:, None, None] * earlier[1])


def pass_states(written_states, read_states, decays):
    zeros_state = jnp.zeros_like(written_states[0])
    ones_decay = jnp.ones_like(decays[0])

    def chain_step(carried_in, entries):
        running, product_decay = carried_in
        written, factor = entries
        return (
            (written + factor[:, None, None] * running, product_decay * factor),
            (running, product_decay),
        )

    (front_total, front_decay), (front_local, front_prefix) = lax.scan(
        chain_step, (zeros_state, ones_decay), (written_states, decays)
    )
    entering = entering_2(
        (front_decay, front_total), "ctx", combine, (ones_decay, zeros_state), False
    )
    state_in = front_local + front_prefix[:, :, None, None] * entering[1][None]
    (back_total, back_decay), (back_local, back_suffix) = lax.scan(
        chain_step, (zeros_state, ones_decay), (read_states, decays), reverse=True
    )
    leaving = entering_2((back_decay, back_total), "ctx", combine, (ones_decay, zeros_state), True)
    grad_leave = back_local + back_suffix[:, :, None, None] * leaving[1][None]
    return (state_in, grad_leave)


def split_blocks(matrix):
    return matrix.reshape(matrix.shape[0] // BLOCK, BLOCK, matrix.shape[1])


def flatten_blocks(matrix):
    return matrix.reshape(matrix.shape[0] * matrix.shape[1], matrix.shape[2])


def local_work(inputs, out_grad, keys, queries, decay, mask_values, exchanged):
    blocks = (
        split_blocks(inputs),
        split_blocks(out_grad),
        split_blocks(keys),
        split_blocks(queries),
    )
    levels = jnp.cumsum(split_blocks(decay), axis=1)
    written_states, read_states, decays = lax.map(block_summary, blocks + (levels,))
    state_in, grad_leave = exchanged(written_states, read_states, decays)
    results = lax.map(
        partial(block_grads, mask_values=mask_values), blocks + (levels, state_in, grad_leave)
    )
    return tuple((flatten_blocks(result) for result in results))


def states_in_place(written_states, read_states, decays):
    return pass_states(written_states, read_states, decays)


def per_device(inputs, out_grad, input_map, output_map, log_decay, block_mask):
    mask_values = block_mask.astype(jnp.float32)
    moved_inputs, moved_grads, moved_keys, moved_query = (
        lax.all_to_all(inputs, "head", split_axis=1, concat_axis=0, tiled=True),
        lax.all_to_all(out_grad, "head", split_axis=1, concat_axis=0, tiled=True),
        lax.all_to_all(input_map, "head", split_axis=1, concat_axis=0, tiled=True),
        lax.all_to_all(output_map, "head", split_axis=1, concat_axis=0, tiled=True),
    )
    moved_decay = lax.all_to_all(
        log_decay.astype(jnp.bfloat16), "head", split_axis=1, concat_axis=0, tiled=True
    ).astype(log_decay.dtype)
    grad_in, grad_keys, grad_query, grad_decay = local_work(
        moved_inputs,
        moved_grads,
        moved_keys,
        moved_query,
        moved_decay,
        mask_values,
        states_in_place,
    )
    grad_in, grad_keys, grad_query = (
        lax.all_to_all(
            grad_in.astype(jnp.bfloat16), "head", split_axis=0, concat_axis=1, tiled=True
        ),
        lax.all_to_all(
            grad_keys.astype(jnp.bfloat16), "head", split_axis=0, concat_axis=1, tiled=True
        ),
        lax.all_to_all(
            grad_query.astype(jnp.bfloat16), "head", split_axis=0, concat_axis=1, tiled=True
        ),
    )
    grad_decay = lax.all_to_all(grad_decay, "head", split_axis=0, concat_axis=1, tiled=True)
    return (grad_in, grad_keys, grad_query, grad_decay)


def solution(mesh):
    in_specs = (
        P(("ctx", "head"), None),
        P(("ctx", "head"), None),
        P(("ctx", "head"), None),
        P(("ctx", "head"), None),
        P(("ctx", "head"), None),
        P(),
    )
    out_specs = (
        P(("ctx", "head"), None),
        P(("ctx", "head"), None),
        P(("ctx", "head"), None),
        P(("ctx", "head"), None),
    )
    return jax.shard_map(
        per_device, mesh=mesh, in_specs=in_specs, out_specs=out_specs, check_vma=False
    )
```

profile of v0, /device:TPU:0, one launch (start us, length us, event | category | flops | bytes accessed | tf_op | source)
XLA Modules:
  0.0 1032.4 jit_solution(2628855568259976157)
XLA Ops:
  8.8 4.4 all-to-all-start.1
  15.2 3.6 all-to-all-done.1
  24.4 6.2 all-to-all-done.2
  34.1 6.4 copy.224
  42.9 4.8 all-to-all-start
  47.8 6.4 copy.232
  54.2 39.0 %all-to-all-done = bf16[256,4,2048]{0,2,1:T(8,128)(2,1)} async-done(((bf16[256,4,2048]{0,2,1:T(8,128)(2,1)}), bf16[256,4,2048]{0,2,1:T(8,128)(2,1)}, u32[]{:S(2)}, u32[]{:S(2)}) %all-to-all-start) | async-done | bytes 4194336 | tf_op jit(solution)/shard_map/all_to_all | solution.py:223
  93.2 4.9 all-to-all-start.4
  104.3 38.3 %all-to-all-done.4 = bf16[256,4,2048]{0,2,1:T(8,128)(2,1)} async-done(((bf16[256,4,2048]{0,2,1:T(8,128)(2,1)}), bf16[256,4,2048]{0,2,1:T(8,128)(2,1)}, u32[]{:S(2)}, u32[]{:S(2)}) %all-to-all-start.4) | async-done | bytes 4194336 | tf_op jit(solution)/shard_map/all_to_all | solution.py:222
  142.6 33.1 %while.98 = (s32[]{:T(128)}, f32[4,32,128,64]{2,3,1,0:T(8,128)}, f32[4,32,128,64]{2,3,1,0:T(8,128)}, f32[4,32]{1,0:T(4,128)S(1)}, f32[4,256,32]{2,1,0:T(8,128)S(...) while((s32[]{:T(128)}, f32[4,32,128,64]{2,3,1,0:T(8,128)}, ...), condition=%wide.region_3.4_spmd, body=%wide.region_2.3_spmd.sunk | while | flops 1613242368 | bytes 17860128 | solution.py:207
  175.7 4.2 broadcast.87.clone.2
  179.9 27.3 %while.103 = (s32[]{:T(128)}, f32[32,128,64]{2,1,0:T(8,128)S(1)}, f32[32]{0:T(128)S(1)}, f32[4,32,128,64]{3,2,1,0:T(8,128)}, f32[4,32]{1,0:T(4,128)S(1)}, /*inde...) while((s32[]{:T(128)}, f32[32,128,64]{2,1,0:T(8,128)S(1)}, ...), condition=%wide.region_5.6_spmd.clone, body=%wide.region_4.5_spmd.clone.sunk | while | flops 1048643 | bytes 10487413 | solution.py:176
  209.0 4.3 broadcast.87.clone.1
  213.3 27.5 %while.102 = (s32[]{:T(128)}, f32[32,128,64]{2,1,0:T(8,128)S(1)}, f32[32]{0:T(128)S(1)}, f32[4,32,128,64]{3,2,1,0:T(8,128)}, f32[4,32]{1,0:T(4,128)S(1)}, /*inde...) while((s32[]{:T(128)}, f32[32,128,64]{2,1,0:T(8,128)S(1)}, ...), condition=%wide.region_9.10_spmd.clone, body=%wide.region_8.9_spmd.clone.sunk | while | flops 1048644 | bytes 10486925 | solution.py:183
  244.9 69.0 %all-reduce.2 = (f32[1024]{0:T(1024)S(1)}, f32[1024]{0:T(1024)S(1)}) all-reduce(f32[1024]{0:T(1024)S(1)} %dynamic-update-slice.12, f32[1024]{0:T(1024)S(1)} %dynamic-update-slice.13), channel_id=3, replica_groups=mesh['ctx'=32,'head'=4] {'ctx'}, use_global_device_ids=true, to_apply=%add | all-reduce | flops 2048 | bytes 16384
  314.1 10.7 %all-gather.9.cloned.1.call-done = f32[1024,128,64]{1,2,0:T(8,128)} async-done(((f32[32,128,64]{1,2,0:T(8,128)}), f32[1024,128,64]{1,2,0:T(8,128)}) %all-gather.9.cloned.1.call-update) | async-done | bytes 33554448 | tf_op jit(solution)/shard_map/all_gather | solution.py:22
  326.6 7.9 multiply_add_fusion
  334.5 7.2 copy.248
  341.6 98.0 %all-gather.7.cloned.1.call-done = f32[1024,128,64]{1,2,0:T(8,128)} async-done(((f32[32,128,64]{1,2,0:T(8,128)}), f32[1024,128,64]{1,2,0:T(8,128)}) %all-gather.7.cloned.1.call-update) | async-done | bytes 33554448 | tf_op jit(solution)/shard_map/all_gather | solution.py:22
  441.2 158.2 %while.99 = (s32[]{:T(128)}, f32[32,128,64]{2,1,0:T(8,128)}, s32[]{:T(128)}, f32[32,32,128,64]{2,3,1,0:T(8,128)}, f32[32,32]{1,0:T(8,128)S(1)}, /*index=5*/s32[]{:T(128)}, s32[]{:T(128)}, s32[]{:T(128)}, s32[]{:T(128)}) while((s32[]{:T(128)}, f32[32,128,64]{2,1,0:T(8,128)}, s32[]{:T(128)}, f32[32,32,128,64]{2,3,1,0:T(8,128)}, ...), condition=%wide.region_11.12_spmd, body=%wide.region_10.11_spmd.sunk | while | flops 524294 | bytes 7340563 | solution.py:31
  599.5 7.9 multiply_add_fusion.1
  607.4 6.8 copy.247
  614.2 325.8 %while.101 = (s32[]{:T(128)}, bf16[4,256,2048]{1,2,0:T(8,128)(2,1)}, bf16[4,256,256]{1,2,0:T(8,128)(2,1)}, bf16[4,256,256]{1,2,0:T(8,128)(2,1)}, f32[4,256,32]{1...) while((s32[]{:T(128)}, bf16[4,256,2048]{1,2,0:T(8,128)(2,1)}, ...), condition=%wide.region_29.30_spmd, body=%wide.region_12.29_spmd.sunk | while | flops 5584830464 | bytes 82941960 | solution.py:209
  625.5 4.0 fusion.216
  629.5 3.6 convolution_bitcast_fusion.21
  644.9 4.2 multiply_reduce_fusion.17
  653.2 4.4 multiply_reduce_fusion.15
  706.9 4.0 fusion.216
  710.9 3.6 convolution_bitcast_fusion.21
  726.3 4.2 multiply_reduce_fusion.17
  734.6 4.4 multiply_reduce_fusion.15
  769.2 3.6 fusion.222
  788.3 4.0 fusion.216
  792.3 3.6 convolution_bitcast_fusion.21
  807.7 4.2 multiply_reduce_fusion.17
  816.0 4.4 multiply_reduce_fusion.15
  850.6 3.6 fusion.222
  869.7 4.0 fusion.216
  873.7 3.6 convolution_bitcast_fusion.21
  889.1 4.2 multiply_reduce_fusion.17
  897.4 4.4 multiply_reduce_fusion.15
  932.0 3.6 fusion.222
  940.1 10.2 all_to_all.141
  950.3 11.5 %all_to_all.142 = bf16[4,256,256]{1,2,0:T(8,128)(2,1)S(1)} all-to-all(bf16[4,256,256]{1,2,0:T(8,128)(2,1)} %get-tuple-element.568), channel_id=1, replica_groups=mesh['ctx'=32,'head'=4] {'head'}, dimensions={0} | all-to-all | bytes 1048576 | tf_op jit(solution)/shard_map/all_to_all | solution.py:243
  961.8 11.5 %all_to_all.143 = bf16[4,256,256]{1,2,0:T(8,128)(2,1)S(1)} all-to-all(bf16[4,256,256]{1,2,0:T(8,128)(2,1)} %get-tuple-element.569), channel_id=1, replica_groups=mesh['ctx'=32,'head'=4] {'head'}, dimensions={0} | all-to-all | bytes 1048576 | tf_op jit(solution)/shard_map/all_to_all | solution.py:246
  973.3 4.9 all-to-all-start.5
  980.9 38.0 %all-to-all-done.5 = bf16[4,256,2048]{1,2,0:T(8,128)(2,1)} async-done(((bf16[4,256,2048]{1,2,0:T(8,128)(2,1)}), bf16[4,256,2048]{1,2,0:T(8,128)(2,1)}, u32[]{:S(2)}, u32[]{:S(2)}) %all-to-all-start.5) | async-done | bytes 4194336 | tf_op jit(solution)/shard_map/all_to_all | solution.py:240
  1018.9 6.3 copy.269
  (687 shorter events, 526.6 us)
Async XLA Ops:
  8.8 10.0 all-to-all-start.1
  18.8 11.8 %all-to-all-start.2 = ((bf16[256,4,256]{0,2,1:T(8,128)(2,1)}), bf16[256,4,256]{0,2,1:T(8,128)(2,1)S(1)}, u32[]{:S(2)}, u32[]{:S(2)}) async-start(bf16[256,4,256]{0,2,1:T(8,128)(2,1)} %bitcast.89), calls=%async_computation.2 | async-start | bytes 1048576 | tf_op jit(solution)/shard_map/all_to_all | solution.py:225
  30.6 9.9 copy-start.14
  30.6 11.5 %all-to-all-start.3 = ((bf16[256,4,256]{0,2,1:T(8,128)(2,1)}), bf16[256,4,256]{0,2,1:T(8,128)(2,1)S(1)}, u32[]{:S(2)}, u32[]{:S(2)}) async-start(bf16[256,4,256]{0,2,1:T(8,128)(2,1)} %bitcast.91), calls=%async_computation.3 | async-start | bytes 1048576 | tf_op jit(solution)/shard_map/all_to_all | solution.py:224
  42.9 50.3 %all-to-all-start = ((bf16[256,4,2048]{0,2,1:T(8,128)(2,1)}), bf16[256,4,2048]{0,2,1:T(8,128)(2,1)}, u32[]{:S(2)}, u32[]{:S(2)}) async-start(bf16[256,4,2048]{0,2,1:T(8,128)(2,1)} %bitcast.494), calls=%async_computation | async-start | bytes 8388608 | tf_op jit(solution)/shard_map/all_to_all | solution.py:223
  93.2 49.4 %all-to-all-start.4 = ((bf16[256,4,2048]{0,2,1:T(8,128)(2,1)}), bf16[256,4,2048]{0,2,1:T(8,128)(2,1)}, u32[]{:S(2)}, u32[]{:S(2)}) async-start(bf16[256,4,2048]{0,2,1:T(8,128)(2,1)} %bitcast.493), calls=%async_computation.4 | async-start | bytes 8388608 | tf_op jit(solution)/shard_map/all_to_all | solution.py:222
  98.1 226.7 %all-gather.9.cloned.1.call-start = ((), (), s32[]{:S(2)}) async-start(), calls=%async_computation.10 | async-start | bytes 34603008 | tf_op jit(solution)/shard_map/all_gather | solution.py:22
  175.7 4.3 copy-start.12
  175.7 4.3 copy-start.13
  208.9 230.8 %all-gather.7.cloned.1.call-start = ((), (), s32[]{:S(2)}) async-start(), calls=%async_computation.9 | async-start | bytes 34603008 | tf_op jit(solution)/shard_map/all_gather | solution.py:22
  643.8 5.3 copy-start.16
  644.0 5.1 copy-start.8
  653.0 4.6 copy-start.17
  653.2 4.4 copy-start.10
  674.9 12.3 %copy-start.2 = (f32[1,16,128,64]{2,3,1,0:T(8,128)S(1)}, f32[1,16,128,64]{2,3,1,0:T(8,128)}, u32[]{:S(2)}) copy-start(f32[1,16,128,64]{2,3,1,0:T(8,128)} %copy-done.1) | copy-start | bytes 1572868 | tf_op jit(solution)/shard_map/while
  677.2 10.5 %copy-start.5 = (bf16[256,1024]{0,1:T(8,128)(2,1)S(1)}, bf16[256,1024]{0,1:T(8,128)(2,1)}, u32[]{:S(2)}) copy-start(bf16[256,1024]{0,1:T(8,128)(2,1)} %copy-done.4) | copy-start | bytes 1572868 | tf_op jit(solution)/shard_map/while
  681.2 6.6 copy-start.9
  681.2 6.6 copy-start.20
  686.5 4.9 copy-start
  725.2 5.3 copy-start.16
  725.4 5.1 copy-start.8
  734.4 4.6 copy-start.17
  734.6 4.4 copy-start.10
  756.3 12.3 %copy-start.2 = (f32[1,16,128,64]{2,3,1,0:T(8,128)S(1)}, f32[1,16,128,64]{2,3,1,0:T(8,128)}, u32[]{:S(2)}) copy-start(f32[1,16,128,64]{2,3,1,0:T(8,128)} %copy-done.1) | copy-start | bytes 1572868 | tf_op jit(solution)/shard_map/while
  758.6 10.5 %copy-start.5 = (bf16[256,1024]{0,1:T(8,128)(2,1)S(1)}, bf16[256,1024]{0,1:T(8,128)(2,1)}, u32[]{:S(2)}) copy-start(bf16[256,1024]{0,1:T(8,128)(2,1)} %copy-done.4) | copy-start | bytes 1572868 | tf_op jit(solution)/shard_map/while
  762.6 6.6 copy-start.9
  762.6 6.6 copy-start.20
  767.9 4.9 copy-start
  769.2 4.2 copy-start.3
  806.6 5.3 copy-start.16
  806.8 5.1 copy-start.8
  815.8 4.6 copy-start.17
  816.0 4.4 copy-start.10
  837.7 12.3 %copy-start.2 = (f32[1,16,128,64]{2,3,1,0:T(8,128)S(1)}, f32[1,16,128,64]{2,3,1,0:T(8,128)}, u32[]{:S(2)}) copy-start(f32[1,16,128,64]{2,3,1,0:T(8,128)} %copy-done.1) | copy-start | bytes 1572868 | tf_op jit(solution)/shard_map/while
  840.1 10.5 %copy-start.5 = (bf16[256,1024]{0,1:T(8,128)(2,1)S(1)}, bf16[256,1024]{0,1:T(8,128)(2,1)}, u32[]{:S(2)}) copy-start(bf16[256,1024]{0,1:T(8,128)(2,1)} %copy-done.4) | copy-start | bytes 1572868 | tf_op jit(solution)/shard_map/while
  844.0 6.6 copy-start.9
  844.0 6.6 copy-start.20
  849.3 4.9 copy-start
  888.0 5.3 copy-start.16
  888.2 5.1 copy-start.8
  897.2 4.6 copy-start.17
  897.4 4.4 copy-start.10
  919.1 12.3 %copy-start.2 = (f32[1,16,128,64]{2,3,1,0:T(8,128)S(1)}, f32[1,16,128,64]{2,3,1,0:T(8,128)}, u32[]{:S(2)}) copy-start(f32[1,16,128,64]{2,3,1,0:T(8,128)} %copy-done.1) | copy-start | bytes 1572868 | tf_op jit(solution)/shard_map/while
  921.5 10.5 %copy-start.5 = (bf16[256,1024]{0,1:T(8,128)(2,1)S(1)}, bf16[256,1024]{0,1:T(8,128)(2,1)}, u32[]{:S(2)}) copy-start(bf16[256,1024]{0,1:T(8,128)(2,1)} %copy-done.4) | copy-start | bytes 1572868 | tf_op jit(solution)/shard_map/while
  925.4 6.6 copy-start.9
  925.4 6.6 copy-start.20
  930.7 4.9 copy-start
  973.3 45.6 %all-to-all-start.5 = ((bf16[4,256,2048]{1,2,0:T(8,128)(2,1)}), bf16[4,256,2048]{1,2,0:T(8,128)(2,1)}, u32[]{:S(2)}, u32[]{:S(2)}) async-start(bf16[4,256,2048]{1,2,0:T(8,128)(2,1)} %get-tuple-element.567), calls=%async_computation.5 | async-start | bytes 8388608 | tf_op jit(solution)/shard_map/all_to_all | solution.py:240
  (30 other events, 86.6 us)
Sparse Core Ops, SparseCore 0:
  209.0 115.7 all-gather.8
  327.1 112.5 all-gather.6
where the time goes:
time: 1050 us; the launch traced here: 1030 us
  local copies, waits for them, and re-layouts  257 us (24%)
  waiting for transfers between devices  236 us (22%)
  other arithmetic  212 us (20%)
  matrix products  181 us (17%)
  blocking collectives  102 us (10%)
  starting transfers between devices  26 us (2%)
  between operations  15.3 us (1%)
    all_gather x2, waiting for transfers between devices, entering_2(): gathered = jax.tree.map(lambda a: lax.all_gather(a, axis), part)  109 us
    add x31, other arithmetic, combine(): latter[1] + latter[0][:, None, None] * earlier[1]  98.4 us
    dot_general x40, matrix products, product_two(): jnp.einsum(form, first, second, precision=HIGHEST_PRECISION, preferred_el...  95.9 us
    unnamed x1, blocking collectives  69 us
    dynamic_slice x62, local copies, waits for them, and re-layouts, one(): lax.dynamic_index_in_dim(a, source, 0, False)  58.8 us
    all_to_all x1, waiting for transfers between devices, per_device(): lax.all_to_all(out_grad, 'head', split_axis=1, concat_axis=0, tiled=True)  39 us
    all_to_all x1, waiting for transfers between devices, per_device(): lax.all_to_all(inputs, 'head', split_axis=1, concat_axis=0, tiled=True)  38.3 us
    all_to_all x1, waiting for transfers between devices, per_device(): lax.all_to_all(grad_in.astype(jnp.bfloat16), 'head', split_axis=0, concat...  38 us
  transfers between devices with their start and end apart: 8, of which 8 were waited for; matrix products, arithmetic and copies ran while one was open for 8% of the time, Pallas kernels for 0%

commit v1 on v0

v1 whole, which is shorter than its diff:
```python
import jax
import jax.numpy as jnp
from jax import lax
from jax.experimental import pallas as pl
from jax.experimental.pallas import tpu as pltpu
from jax.sharding import PartitionSpec as P

HEAD_COUNT = 128
HEAD_DIM = 64
STATE = 128
GROUPS = 8
BLOCK = 256
FEATURES = HEAD_COUNT * HEAD_DIM
SPAN = FEATURES // GROUPS
PER_GROUP = HEAD_COUNT // GROUPS
HALF = BLOCK // 2
DEVICES = 128
PIECE_COLS = 512
AXES = ("ctx", "head")
F32 = jnp.float32
BF16 = jnp.bfloat16


def dot(a, b, ca=1, cb=0):
    return lax.dot_general(a, b, (((ca,), (cb,)), ((), ())), preferred_element_type=F32)


def split_two(a):
    high = a.astype(BF16)
    return high, (a - high.astype(F32)).astype(BF16)


def split_three(a):
    high = a.astype(BF16)
    rest = a - high.astype(F32)
    mid = rest.astype(BF16)
    return high, mid, (rest - mid.astype(F32)).astype(BF16)


def exact_dot(selector, a):
    high, mid, low = split_three(a)
    return (dot(selector, low) + dot(selector, mid)) + dot(selector, high)


def spread(a, chooser):
    high, mid, low = split_three(a)
    return (dot(low, chooser) + dot(mid, chooser)) + dot(high, chooser)


def head_chooser(first_head, cols):
    rows = lax.broadcasted_iota(jnp.int32, (HEAD_COUNT, cols), 0)
    owner = lax.broadcasted_iota(jnp.int32, (HEAD_COUNT, cols), 1) // HEAD_DIM + first_head
    return (rows == owner).astype(F32).astype(BF16)


def triangle(lower):
    rows = lax.broadcasted_iota(jnp.int32, (BLOCK, BLOCK), 0)
    cols = lax.broadcasted_iota(jnp.int32, (BLOCK, BLOCK), 1)
    keep = rows >= cols if lower else rows <= cols
    return keep.astype(F32).astype(BF16)


def summary_kernel(x_ref, dy_ref, b_ref, c_ref, decay_ref, f_ref, r_ref, level_ref):
    g = pl.program_id(0)

    @pl.when(g == 0)
    def _():
        level_ref[...] = exact_dot(triangle(True), decay_ref[...])

    level = spread(level_ref[...], head_chooser(g * PER_GROUP, SPAN))
    closing = jnp.exp(level[BLOCK - 1 :] - level)
    opening = jnp.exp(level)
    for coef, val_ref, map_ref, out_ref in (
        (closing, x_ref, b_ref, f_ref),
        (opening, dy_ref, c_ref, r_ref),
    ):
        high, low = split_two(coef * val_ref[...].astype(F32))
        turned = map_ref[...].T
        state = (dot(turned, low) + dot(turned, high)).astype(BF16)
        for c in range(SPAN // PIECE_COLS):
            for n in range(STATE // 16):
                out_ref[c, n] = state[
                    n * 16 : (n + 1) * 16, c * PIECE_COLS : (c + 1) * PIECE_COLS
                ]


def inside_kernel(
    x_ref, dy_ref, b_ref, c_ref, level_ref, mask_ref, gx_ref, gb_ref, gc_ref, gl_ref, y_ref
):
    g = pl.program_id(0)
    chooser = head_chooser(g * PER_GROUP, SPAN)
    level = spread(level_ref[...], chooser)
    for i, (t, s) in enumerate(((0, 0), (1, 1), (1, 0))):
        ts = pl.ds(t * HALF, HALF)
        ss = pl.ds(s * HALF, HALF)
        at = t * HALF + HALF // 2 if t == s else HALF - 1
        ref_level = level[at : at + 1]
        a = jnp.exp(level[t * HALF : (t + 1) * HALF] - ref_level)
        b = jnp.exp(ref_level - level[s * HALF : (s + 1) * HALF])
        u = (a * dy_ref[ts, :].astype(F32)).astype(BF16)
        v = (b * x_ref[ss, :].astype(F32)).astype(BF16)
        keep = mask_ref[ts, ss] == 1
        bs = b_ref[ss, :]
        ct = c_ref[ts, :]
        scores = jnp.where(keep, dot(ct, bs, 1, 1), 0.0)
        together = jnp.where(keep, dot(u, v, 1, 1), 0.0)
        score_n = scores.astype(BF16)
        score_t = scores.T.astype(BF16)
        high, low = split_two(together)
        high_t, low_t = split_two(together.T)
        gc = dot(low, bs) + dot(high, bs)
        gb = dot(low_t, ct) + dot(high_t, ct)
        y = a * dot(score_n, v)
        gx = b * dot(score_t, u)
        if i < 2:
            gc_ref[ts, :] = gc
            gb_ref[ss, :] = gb
            y_ref[ts, :] = y
            gx_ref[ss, :] = gx
        else:
            gc_ref[ts, :] += gc
            gb_ref[ss, :] += gb
            y_ref[ts, :] += y
            gx_ref[ss, :] += gx
    term = dy_ref[...].astype(F32) * y_ref[...] - x_ref[...].astype(F32) * gx_ref[...]
    high, low = split_two(term)
    total = dot(low, chooser, 1, 1) + dot(high, chooser, 1, 1)

    @pl.when(g == 0)
    def _():
        gl_ref[...] = total

    @pl.when(g > 0)
    def _():
        gl_ref[...] += total


def scan_kernel(f_ref, r_ref, decay_ref, s_ref, g_ref, wide_ref):
    owner = lax.axis_index("ctx") * 4 + lax.axis_index("head")
    first = (owner // 8) * (PIECE_COLS // HEAD_DIM)
    wide_ref[...] = jnp.exp(spread(decay_ref[...], head_chooser(first, PIECE_COLS)))

    def step(i, carry):
        front, back = carry
        j = DEVICES - 1 - i
        s_ref[i] = front.astype(BF16)
        g_ref[j] = back.astype(BF16)
        front = wide_ref[pl.ds(i, 1), :] * front + f_ref[i].astype(F32)
        back = wide_ref[pl.ds(j, 1), :] * back + r_ref[j].astype(F32)
        return front, back

    zero = jnp.zeros((16, PIECE_COLS), F32)
    lax.fori_loop(0, DEVICES, step, (zero, zero), unroll=8)


def finish_kernel(
    x_ref, dy_ref, b_ref, c_ref, level_ref, s_ref, g_ref, gx_in, gb_in, gc_in, gl_in,
    gx_ref, gb_ref, gc_ref, gd_ref, gl_ref,
):
    g = pl.program_id(0)
    chooser = head_chooser(g * PER_GROUP, SPAN)
    level = spread(level_ref[...], chooser)
    closing = jnp.exp(level[BLOCK - 1 :] - level)
    opening = jnp.exp(level)

    def whole(ref):
        return jnp.concatenate(
            [
                jnp.concatenate([ref[c, n] for n in range(STATE // 16)], axis=0)
                for c in range(SPAN // PIECE_COLS)
            ],
            axis=1,
        )

    state = whole(s_ref)
    leave = whole(g_ref)
    od = opening * dy_ref[...].astype(F32)
    gc_ref[...] = (gc_in[...] + dot(od.astype(BF16), state, 1, 1)).astype(BF16)
    row = od * dot(c_ref[...], state)
    cx = closing * x_ref[...].astype(F32)
    gb_ref[...] = (gb_in[...] + dot(cx.astype(BF16), leave, 1, 1)).astype(BF16)
    back = dot(b_ref[...], leave)
    gx_ref[...] = (gx_in[...] + closing * back).astype(BF16)
    col = cx * back
    last = jnp.sum(col, axis=0, keepdims=True) + jnp.exp(level[BLOCK - 1 :]) * jnp.sum(
        state.astype(F32) * leave.astype(F32), axis=0, keepdims=True
    )
    is_last = lax.broadcasted_iota(jnp.int32, (BLOCK, SPAN), 0) == BLOCK - 1
    high, low = split_two((row - col) + jnp.where(is_last, last, 0.0))
    total = dot(low, chooser, 1, 1) + dot(high, chooser, 1, 1)

    @pl.when(g == 0)
    def _():
        gl_ref[...] = gl_in[...] + total

    @pl.when(g > 0)
    def _():
        gl_ref[...] += total

    @pl.when(g == GROUPS - 1)
    def _():
        gd_ref[...] = exact_dot(triangle(False), gl_ref[...])


def per_device(inputs, out_grad, input_map, output_map, log_decay, block_mask):
    wide = pl.BlockSpec((BLOCK, SPAN), lambda g: (0, g))
    thin = pl.BlockSpec((BLOCK, STATE), lambda g: (0, g))
    heads = pl.BlockSpec((BLOCK, HEAD_COUNT), lambda g: (0, 0))
    square = pl.BlockSpec((BLOCK, BLOCK), lambda g: (0, 0))
    pieces = pl.BlockSpec((SPAN // PIECE_COLS, STATE // 16, 16, PIECE_COLS), lambda g: (g, 0, 0, 0))
    piece_shape = (FEATURES // PIECE_COLS, STATE // 16, 16, PIECE_COLS)
    params = pltpu.CompilerParams(vmem_limit_bytes=56 * 1024 * 1024)
    f, r, level = pl.pallas_call(
        summary_kernel,
        grid=(GROUPS,),
        in_specs=[wide, wide, thin, thin, heads],
        out_specs=[pieces, pieces, heads],
        out_shape=[
            jax.ShapeDtypeStruct(piece_shape, BF16),
            jax.ShapeDtypeStruct(piece_shape, BF16),
            jax.ShapeDtypeStruct((BLOCK, HEAD_COUNT), F32),
        ],
        compiler_params=params,
    )(inputs, out_grad, input_map, output_map, log_decay)
    ends = lax.all_to_all(
        jnp.broadcast_to(level[BLOCK - 1 :], (DEVICES, HEAD_COUNT)), AXES, 0, 0, tiled=True
    )
    flat = (DEVICES, 16, PIECE_COLS)
    sent = jnp.concatenate([f.reshape(flat), r.reshape(flat)], axis=1)
    came = lax.all_to_all(sent, AXES, 0, 0, tiled=True)
    came_f, came_r = came[:, :16], came[:, 16:]
    gx_in, gb_in, gc_in, gl_in = pl.pallas_call(
        inside_kernel,
        grid=(GROUPS,),
        in_specs=[wide, wide, thin, thin, heads, square],
        out_specs=[wide, thin, thin, heads],
        out_shape=[
            jax.ShapeDtypeStruct((BLOCK, FEATURES), F32),
            jax.ShapeDtypeStruct((BLOCK, GROUPS * STATE), F32),
            jax.ShapeDtypeStruct((BLOCK, GROUPS * STATE), F32),
            jax.ShapeDtypeStruct((BLOCK, HEAD_COUNT), F32),
        ],
        scratch_shapes=[pltpu.VMEM((BLOCK, SPAN), F32)],
        compiler_params=params,
    )(inputs, out_grad, input_map, output_map, level, block_mask)
    s, g = pl.pallas_call(
        scan_kernel,
        out_shape=[jax.ShapeDtypeStruct(flat, BF16), jax.ShapeDtypeStruct(flat, BF16)],
        scratch_shapes=[pltpu.VMEM((DEVICES, PIECE_COLS), F32)],
        compiler_params=params,
    )(came_f, came_r, ends)
    back = lax.all_to_all(jnp.concatenate([s, g], axis=1), AXES, 0, 0, tiled=True)
    s, g = back[:, :16].reshape(piece_shape), back[:, 16:].reshape(piece_shape)
    return pl.pallas_call(
        finish_kernel,
        grid=(GROUPS,),
        in_specs=[wide, wide, thin, thin, heads, pieces, pieces, wide, thin, thin, heads],
        out_specs=[wide, thin, thin, heads],
        out_shape=[
            jax.ShapeDtypeStruct((BLOCK, FEATURES), BF16),
            jax.ShapeDtypeStruct((BLOCK, GROUPS * STATE), BF16),
            jax.ShapeDtypeStruct((BLOCK, GROUPS * STATE), BF16),
            jax.ShapeDtypeStruct((BLOCK, HEAD_COUNT), F32),
        ],
        scratch_shapes=[pltpu.VMEM((BLOCK, HEAD_COUNT), F32)],
        compiler_params=params,
    )(inputs, out_grad, input_map, output_map, level, s, g, gx_in, gb_in, gc_in, gl_in)


def solution(mesh):
    split = P(AXES, None)
    return tuple_map(mesh, split)


def tuple_map(mesh, split):
    return jax.shard_map(
        per_device,
        mesh=mesh,
        in_specs=(split, split, split, split, split, P()),
        out_specs=(split, split, split, split),
        check_vma=False,
    )
```

time: 1050 us -> 193 us (0.18); the launches traced: 1030 us -> 192 us
  local copies, waits for them, and re-layouts: 257 us -> 11.3 us
  other arithmetic: 212 us -> 9.55 us
  matrix products: 181 us -> 0 us
  waiting for transfers between devices: 236 us -> 81.3 us
  blocking collectives: 102 us -> 0 us
  Pallas kernels: 0 us -> 66.7 us
  between operations: 15.3 us -> 0.67 us
    dot_general x80 -> x0, matrix products: 161 us -> none  [the longest x40 95.9 us: product_two(): jnp.einsum(form, first, second, precision=HIGHEST_PRECISION, preferred_el...]
    add x45 -> x0, other arithmetic: 134 us -> none  [the longest x31 98.4 us: combine(): latter[1] + latter[0][:, None, None] * earlier[1]]
    all_gather x2 -> x0, waiting for transfers between devices: 109 us -> none  [entering_2(): gathered = jax.tree.map(lambda a: lax.all_gather(a, axis), part)]
    dynamic_slice x86 -> x0, local copies, waits for them, and re-layouts: 85.1 us -> none  [the longest x62 58.8 us: one(): lax.dynamic_index_in_dim(a, source, 0, False)]
    unnamed x1 -> x0, blocking collectives: 69 us -> none
    pallas_call x0 -> x4, Pallas kernels: none -> 66.7 us  [the longest x1 27.3 us: per_device(): pl.pallas_call(inside_kernel, grid=(GROUPS,), in_specs=[wide, wide, thin,...]
    all_to_all x6 -> x3, waiting for transfers between devices: 127 us -> 81.3 us  [the longest x1 51.7 us: per_device(): came = lax.all_to_all(sent, AXES, 0, 0, tiled=True)]
    dynamic_update_slice x28 -> x0, other arithmetic: 33.3 us -> none  [the longest x12 17.8 us: local_work(): lax.map(block_summary, blocks + (levels,))]
  transfers between devices with their start and end apart: 8 -> 3, of which waited for: 8 -> 3; matrix products, arithmetic and copies ran while one was open for 8% -> 3% of each run, Pallas kernels for 0% -> 14%
where the time goes in v1:
time: 193 us; the launch traced here: 192 us
  waiting for transfers between devices  81.3 us (42%)
  Pallas kernels  66.7 us (35%)
  starting transfers between devices  22.1 us (11%)
  local copies, waits for them, and re-layouts  11.3 us (6%)
  other arithmetic  9.55 us (5%)
    all_to_all x1, waiting for transfers between devices, per_device(): came = lax.all_to_all(sent, AXES, 0, 0, tiled=True)  51.7 us
    pallas_call x1, Pallas kernels, per_device(): pl.pallas_call(inside_kernel, grid=(GROUPS,), in_specs=[wide, wide, thin,...  27.3 us
    all_to_all x1, waiting for transfers between devices, per_device(): lax.all_to_all(jnp.concatenate([s, g], axis=1), AXES, 0, 0, tiled=True)  25.1 us
    pallas_call x1, Pallas kernels, per_device(): pl.pallas_call(finish_kernel, grid=(GROUPS,), in_specs=[wide, wide, thin,...  20.6 us
    pallas_call x1, Pallas kernels, per_device(): pl.pallas_call(summary_kernel, grid=(GROUPS,), in_specs=[wide, wide, thin...  13.4 us
    all_to_all x1, starting transfers between devices, per_device(): came = lax.all_to_all(sent, AXES, 0, 0, tiled=True)  11.7 us
    all_to_all x1, starting transfers between devices, per_device(): lax.all_to_all(jnp.concatenate([s, g], axis=1), AXES, 0, 0, tiled=True)  5.83 us
    pallas_call x1, Pallas kernels, per_device(): pl.pallas_call(scan_kernel, out_shape=[jax.ShapeDtypeStruct(flat, BF16),...  5.46 us
  transfers between devices with their start and end apart: 3, of which 3 were waited for; matrix products, arithmetic and copies ran while one was open for 3% of the time, Pallas kernels for 14%

profile of v1, /device:TPU:0, one launch (start us, length us, event | category | flops | bytes accessed | tf_op | source)
XLA Modules:
  0.0 191.6 jit_solution(774153776913120163)
XLA Ops:
  0.6 13.4 %shard_map.93 = (bf16[16,8,16,512]{3,2,1,0:T(8,128)(2,1)}, bf16[16,8,16,512]{3,2,1,0:T(8,128)(2,1)}, f32[256,128]{1,0:T(8,128)}) custom-call(bf16[256,8192]{1,0:T(8,128)(2,1)} %x_ref.5, bf16[256,8192]{1,0:T(8,128)(2,1)} %dy_ref.5, bf16[256,1024]{1,0:T(8,128)(2,1)} %b_ref.5, bf16[256,1024]{1,0:T(8,128)(2,1)} %c_ref.5, f32[256,128]{1,0:T(8,128)} %decay_ref.1), custom_call_target="tpu_custom_call" | custom-call | tf_op jit(solution)/shard_map/pallas_call | solution.py:213
  14.0 4.8 %pad_maximum_fusion = bf16[128,32,512]{2,1,0:T(8,128)(2,1)} fusion(bf16[128,16,512]{2,1,0:T(8,128)(2,1)} %bitcast.10, bf16[128,16,512]{2,1,0:T(8,128)(2,1)} %bitcast.9), kind=kLoop, calls=%fused_computation | loop fusion | flops 8388608 | bytes 8388608 | tf_op jit(solution)/shard_map/concatenate | solution.py:229
  18.8 11.7 %all-to-all-start = ((bf16[128,32,512]{2,1,0:T(8,128)(2,1)}), bf16[128,32,512]{2,1,0:T(8,128)(2,1)}, u32[]{:S(2)}, u32[]{:S(2)}) async-start(bf16[128,32,512]{2,1,0:T(8,128)(2,1)} %pad_maximum_fusion), calls=%async_computation | async-start | bytes 8388608 | tf_op jit(solution)/shard_map/all_to_all | solution.py:230
  30.5 0.7 slice_bitcast_fusion
  31.2 51.7 %all-to-all-done = bf16[128,32,512]{2,1,0:T(8,128)(2,1)} async-done(((bf16[128,32,512]{2,1,0:T(8,128)(2,1)}), bf16[128,32,512]{2,1,0:T(8,128)(2,1)}, u32[]{:S(2)}, u32[]{:S(2)}) %all-to-all-start) | async-done | bytes 4194336 | tf_op jit(solution)/shard_map/all_to_all | solution.py:230
  82.9 0.7 broadcast_in_dim.2
  83.5 4.6 %all-to-all-start.1 = ((f32[128,1,128]{2,1,0:T(1,128)}), f32[128,1,128]{2,1,0:T(1,128)S(1)}, u32[]{:S(2)}, u32[]{:S(2)}) async-start(f32[128,1,128]{2,1,0:T(1,128)} %broadcast_in_dim.2), calls=%async_computation.1 | async-start | bytes 131072 | tf_op jit(solution)/shard_map/all_to_all | solution.py:225
  88.1 4.7 %fusion.1 = (bf16[128,16,512]{2,1,0:T(8,128)(2,1)}, bf16[128,16,512]{2,1,0:T(8,128)(2,1)}) fusion(bf16[128,32,512]{2,1,0:T(8,128)(2,1)} %all-to-all-done), kind=kLoop, calls=%fused_computation.4 | loop fusion | bytes 8388608 | tf_op jit(solution)/shard_map/slice | solution.py:231
  92.8 4.6 %all-to-all-done.1 = f32[128,1,128]{2,1,0:T(1,128)S(1)} async-done(((f32[128,1,128]{2,1,0:T(1,128)}), f32[128,1,128]{2,1,0:T(1,128)S(1)}, u32[]{:S(2)}, u32[]{:S(2)}) %all-to-all-start.1) | async-done | bytes 65568 | tf_op jit(solution)/shard_map/all_to_all | solution.py:225
  97.4 0.0 copy-start
  97.4 0.6 copy-done
  98.0 5.5 %shard_map.94 = (bf16[128,16,512]{2,1,0:T(8,128)(2,1)}, bf16[128,16,512]{2,1,0:T(8,128)(2,1)}) custom-call(bf16[128,16,512]{2,1,0:T(8,128)(2,1)} %get-tuple-element.25.f_ref, bf16[128,16,512]{2,1,0:T(8,128)(2,1)} %get-tuple-element.24.r_ref, f32[128,128]{1,0:T(8,128)} %bitcast.11), custom_call_target="tpu_custom_call" | custom-call | tf_op jit(solution)/shard_map/pallas_call | solution.py:246
  103.5 4.8 %pad_maximum_fusion.1 = bf16[128,32,512]{2,1,0:T(8,128)(2,1)} fusion(bf16[128,16,512]{2,1,0:T(8,128)(2,1)} %get-tuple-element.17, bf16[128,16,512]{2,1,0:T(8,128)(2,1)} %get-tuple-element.16), kind=kLoop, calls=%fused_computation.1 | loop fusion | flops 8388608 | bytes 8388608 | tf_op jit(solution)/shard_map/concatenate | solution.py:252
  108.3 5.8 %all-to-all-start.2 = ((bf16[128,32,512]{2,1,0:T(8,128)(2,1)}), bf16[128,32,512]{2,1,0:T(8,128)(2,1)}, u32[]{:S(2)}, u32[]{:S(2)}) async-start(bf16[128,32,512]{2,1,0:T(8,128)(2,1)} %pad_maximum_fusion.1), calls=%async_computation.2 | async-start | bytes 8388608 | tf_op jit(solution)/shard_map/all_to_all | solution.py:252
  114.1 27.3 %shard_map.95 = (f32[256,8192]{1,0:T(8,128)}, f32[256,1024]{1,0:T(8,128)}, f32[256,1024]{1,0:T(8,128)}, f32[256,128]{1,0:T(8,128)}) custom-call(bf16[256,8192]{1,0:T(8,128)(2,1)} %x_ref.5, bf16[256,8192]{1,0:T(8,128)(2,1)} %dy_ref.5, bf16[256,1024]{1,0:T(8,128)(2,1)} %b_ref.5, bf16[256,1024]{1,0:T(8,128)(2,1)} %c_ref.5, ...), custom_call_target="tpu_custom_call" | custom-call | tf_op jit(solution)/shard_map/pallas_call | solution.py:232
  141.4 25.1 %all-to-all-done.2 = bf16[128,32,512]{2,1,0:T(8,128)(2,1)} async-done(((bf16[128,32,512]{2,1,0:T(8,128)(2,1)}), bf16[128,32,512]{2,1,0:T(8,128)(2,1)}, u32[]{:S(2)}, u32[]{:S(2)}) %all-to-all-start.2) | async-done | bytes 4194336 | tf_op jit(solution)/shard_map/all_to_all | solution.py:252
  166.5 4.6 %fusion = (bf16[128,16,512]{2,1,0:T(8,128)(2,1)}, bf16[128,16,512]{2,1,0:T(8,128)(2,1)}) fusion(bf16[128,32,512]{2,1,0:T(8,128)(2,1)} %all-to-all-done.2), kind=kLoop, calls=%fused_computation.3 | loop fusion | bytes 8388608 | tf_op jit(solution)/shard_map/slice | solution.py:253
  171.1 20.6 %shard_map.96 = (bf16[256,8192]{1,0:T(8,128)(2,1)}, bf16[256,1024]{1,0:T(8,128)(2,1)}, bf16[256,1024]{1,0:T(8,128)(2,1)}, f32[256,128]{1,0:T(8,128)}) custom-call(bf16[256,8192]{1,0:T(8,128)(2,1)} %x_ref.5, bf16[256,8192]{1,0:T(8,128)(2,1)} %dy_ref.5, bf16[256,1024]{1,0:T(8,128)(2,1)} %b_ref.5, bf16[256,1024]{1,0:T(8,128)(2,1)} %c_ref.5, ...), custom_call_target="tpu_custom_call" | custom-call | tf_op jit(solution)/shard_map/pallas_call | solution.py:254
Async XLA Ops:
  18.8 64.1 %all-to-all-start = ((bf16[128,32,512]{2,1,0:T(8,128)(2,1)}), bf16[128,32,512]{2,1,0:T(8,128)(2,1)}, u32[]{:S(2)}, u32[]{:S(2)}) async-start(bf16[128,32,512]{2,1,0:T(8,128)(2,1)} %pad_maximum_fusion), calls=%async_computation | async-start | bytes 8388608 | tf_op jit(solution)/shard_map/all_to_all | solution.py:230
  83.5 13.9 %all-to-all-start.1 = ((f32[128,1,128]{2,1,0:T(1,128)}), f32[128,1,128]{2,1,0:T(1,128)S(1)}, u32[]{:S(2)}, u32[]{:S(2)}) async-start(f32[128,1,128]{2,1,0:T(1,128)} %broadcast_in_dim.2), calls=%async_computation.1 | async-start | bytes 131072 | tf_op jit(solution)/shard_map/all_to_all | solution.py:225
  97.4 0.6 copy-start
  108.3 58.2 %all-to-all-start.2 = ((bf16[128,32,512]{2,1,0:T(8,128)(2,1)}), bf16[128,32,512]{2,1,0:T(8,128)(2,1)}, u32[]{:S(2)}, u32[]{:S(2)}) async-start(bf16[128,32,512]{2,1,0:T(8,128)(2,1)} %pad_maximum_fusion.1), calls=%async_computation.2 | async-start | bytes 8388608 | tf_op jit(solution)/shard_map/all_to_all | solution.py:252
